TPU v7x, 128 devices: a whole 4x4x4 slice. The times are simulated.
128 devices in a mesh: freq: 2 (over core), tile: 64 (over y, x, z).
Axes of the slice: x: 4, y: 4, z: 4, core: 2. Of those that a mesh axis runs over, the one named last changes fastest.
Arguments:
- wave_in: bfloat16 [2, 16384, 2, 256], P(None, 'tile', None, 'freq'), may hold values from -6 to 6
- column_basis: bfloat16 [2, 128, 64, 256, 128], P('freq', None, 'tile'), may hold values from -0.25 to 0.25
- row_basis: bfloat16 [2, 128, 64, 256, 128], P('freq', 'tile'), may hold values from -0.09375 to 0.09375
- tile_scale: float32 [2, 128, 64], P('freq'), may hold values from 0.5 to 2
- tile_ranks: int32 [2, 128, 64], P('freq'), may hold values from 16 to 64, as said below
Outputs:
- forward_out: bfloat16 [2, 32768, 2, 256], P('freq', 'tile')
- adjoint_out: bfloat16 [2, 16384, 2, 256], P(None, 'tile', None, 'freq')
Inputs may be any that keep to these rules, and one draw needn't show every extreme that they name: `tile_ranks`: every entry is a multiple of 16. For each frequency, in each aligned group of 2 tile rows and 1 tile columns the ranks add up to at most 80, and some group reaches that sum.
All inputs are finite; a program needn't handle non-finite values.
Results may differ from a plain program's by a relative error of at most 0.005.
Values may be sent and summed in bfloat16 or wider, within the bound.
A program may use at most 192 MiB of HBM per device.

v0:
```python
import jax
import jax.numpy as jnp
from jax import lax
from jax.sharding import PartitionSpec as P

NB = 256
RMAX = 64
MT_DEV = 2
NT_DEV = 1
NVS = 256


def combine_conj(products):
    shaped = products.reshape(
        products.shape[:-3] + (products.shape[-3] // 32, 2, 16) + products.shape[-2:]
    )
    real_part = shaped[..., 0, :, 0, :] + shaped[..., 1, :, 1, :]
    imag_part = shaped[..., 0, :, 1, :] - shaped[..., 1, :, 0, :]
    return jnp.stack([real_part, imag_part], -3)


def combine_plain(summed):
    real_part = summed[..., 0, 0, :] - summed[..., 1, 1, :]
    imag_part = summed[..., 0, 1, :] + summed[..., 1, 0, :]
    return jnp.stack([real_part, imag_part], -2)


def per_device(wave_in, column_basis, row_basis, tile_scale, tile_ranks):
    tile_count = lax.axis_size("tile")
    my_index = lax.axis_index("tile")
    blocks = RMAX // 16
    base_width = 2 * RMAX
    slot_count = MT_DEV * NT_DEV * blocks
    wavefield = lax.all_to_all(wave_in, "freq", split_axis=0, concat_axis=3, tiled=True)
    column_bases = column_basis[0]
    row_bases = row_basis[0]
    scales = tile_scale[0]
    rank_table = tile_ranks[0]
    live_all = (16 * jnp.arange(blocks, dtype=jnp.int32))[None, None, :] < rank_table[:, :, None]
    weight_all = scales[:, :, None] * live_all.astype(jnp.float32)
    col_weight = lax.dynamic_slice_in_dim(weight_all, my_index * NT_DEV, NT_DEV, 1)
    row_live = lax.dynamic_slice_in_dim(live_all, my_index * MT_DEV, MT_DEV, 0)
    row_weight = lax.dynamic_slice_in_dim(weight_all, my_index * MT_DEV, MT_DEV, 0)
    row_live = jnp.transpose(row_live.reshape(MT_DEV, tile_count, NT_DEV, blocks), (1, 0, 2, 3))
    row_weight = jnp.transpose(row_weight.reshape(MT_DEV, tile_count, NT_DEV, blocks), (1, 0, 2, 3))
    rows_split = row_bases.reshape(MT_DEV, tile_count, NT_DEV, NB, blocks, 2, 16)
    cols_split = column_bases.reshape(tile_count, MT_DEV, NT_DEV, NB, blocks, 2, 16)

    def spread_out(received):
        item_count = received.shape[-1]
        return received.reshape(tile_count, MT_DEV, NT_DEV, blocks, 2, 16, item_count)

    products = jnp.einsum(
        "mjbc,jbpn->mjcpn", column_bases, wavefield, preferred_element_type=jnp.float32
    )
    coded_rows = combine_conj(products) * col_weight[:, :, :, None, None, None]
    coded_rows = coded_rows.astype(jnp.bfloat16).reshape(tile_count, slot_count, 2, 16, NVS)
    summed = jnp.einsum(
        "isjbkqt,sijkptn->ibqpn",
        rows_split,
        spread_out(lax.all_to_all(coded_rows, "tile", split_axis=0, concat_axis=0, tiled=True)),
        preferred_element_type=jnp.float32,
    )
    forward = combine_plain(summed).astype(jnp.bfloat16)
    back_products = jnp.einsum(
        "isjbc,ibpn->sijcpn",
        row_bases.reshape(MT_DEV, tile_count, NT_DEV, NB, base_width),
        forward,
        preferred_element_type=jnp.float32,
    )
    returned = combine_conj(back_products) * row_weight[:, :, :, :, None, None, None]
    returned = returned.astype(jnp.bfloat16).reshape(tile_count, slot_count, 2, 16, NVS)
    summed = jnp.einsum(
        "dijbkqt,dijkptn->jbqpn",
        cols_split,
        spread_out(lax.all_to_all(returned, "tile", split_axis=0, concat_axis=0, tiled=True)),
        preferred_element_type=jnp.float32,
    )
    adjoint = combine_plain(summed).astype(jnp.bfloat16)
    adjoint_out = lax.all_to_all(adjoint, "freq", split_axis=3, concat_axis=0, tiled=True)
    forward_out = forward.reshape(1, MT_DEV * NB, 2, NVS)
    return (forward_out, adjoint_out)


def solution(mesh):
    return jax.shard_map(
        per_device,
        mesh=mesh,
        in_specs=(
            P(None, "tile", None, "freq"),
            P("freq", None, "tile", None, None),
            P("freq", "tile", None, None, None),
            P("freq", None, None),
            P("freq", None, None),
        ),
        out_specs=(P("freq", "tile", None, None), P(None, "tile", None, "freq")),
        check_vma=False,
    )
```

profile of v0, /device:TPU:51, one launch (start us, length us, event | category | flops | bytes accessed | tf_op | source)
XLA Modules:
  0.0 429.9 jit_solution(6152000462999829442)
XLA Ops:
  0.6 4.1 all-to-all-start
  4.8 3.1 compare_select_fusion
  7.8 2.0 copy-done.1
  10.4 17.7 %fusion.4 = f32[2,256,128,128]{1,3,2,0:T(8,128)} fusion(bf16[1,128,1,256,128]{4,3,2,1,0:T(8,128)(2,1)} %param.6, bf16[256,2,256,1]{2,0,1,3:T(8,128)(2,1)S(1)} %reshape.408), kind=kOutput, calls=%fused_computation.10 | convolution fusion | flops 4294967296 | bytes 42205184 | tf_op jit(solution)/shard_map/mjbc,jbpn->mjcpn/dot_general | solution.py:53
  28.1 18.9 %slice_add_fusion = (f32[128,1,4,1,16,1,256]{6,4,3,2,0,5,1:T(8,128)}, f32[128,1,4,1,16,1,256]{6,4,3,2,0,5,1:T(8,128)}) fusion(f32[128,1,4,2,16,2,256]{6,4,3,2,0,5,1:T(8,128)} %bitcast.116), kind=kLoop, calls=%fused_computation.5 | loop fusion | flops 4194304 | bytes 50331648 | tf_op jit(solution)/shard_map/add | solution.py:17
  47.0 9.1 %fusion = bf16[64,8,2,16,256]{4,3,2,1,0:T(8,128)(2,1)} fusion(f32[64,8,1,16,256]{4,3,2,1,0:T(8,128)} %bitcast.121, f32[64,8,1,16,256]{4,3,2,1,0:T(8,128)} %bitcast.120, f32[64,8]{1,0:T(8,128)S(1)} %mul.50), kind=kLoop, calls=%fused_computation.1 | loop fusion | flops 12582912 | bytes 25167872 | tf_op jit(solution)/shard_map/convert_element_type | solution.py:57
  56.1 10.6 %all-to-all-start.1 = ((bf16[64,8,2,16,256]{4,3,2,1,0:T(8,128)(2,1)}), bf16[64,8,2,16,256]{4,3,2,1,0:T(8,128)(2,1)}, u32[]{:S(2)}, u32[]{:S(2)}) async-start(bf16[64,8,2,16,256]{4,3,2,1,0:T(8,128)(2,1)} %fusion), calls=%async_computation.1 | async-start | bytes 16777216 | tf_op jit(solution)/shard_map/all_to_all | solution.py:61
  66.7 12.0 %copy.88 = bf16[1,2,64,256,128]{3,4,2,1,0:T(8,128)(2,1)} copy(bf16[1,2,64,256,128]{4,3,2,1,0:T(8,128)(2,1)} %param.7) | data formatting | bytes 16777216 | tf_op args[2]
  78.7 1.0 constant_dynamic-slice_fusion
  79.9 113.2 %all-to-all-done.1 = bf16[64,8,2,16,256]{4,3,2,1,0:T(8,128)(2,1)} async-done(((bf16[64,8,2,16,256]{4,3,2,1,0:T(8,128)(2,1)}), bf16[64,8,2,16,256]{4,3,2,1,0:T(8,128)(2,1)}, u32[]{:S(2)}, u32[]{:S(2)}) %all-to-all-start.1) | async-done | bytes 8388640 | tf_op jit(solution)/shard_map/all_to_all | solution.py:61
  193.1 11.4 %fusion.9 = f32[2,2,256,256,2,1,1]{2,3,5,0,4,1,6:T(8,128)S(1)} fusion(bf16[2,64,256,4,2,16,1]{2,5,4,3,1,0,6:T(8,128)(2,1)} %bitcast.126, bf16[64,2,4,2,16,256,1]{5,4,3,2,1,0,6:T(8,128)(2,1)} %bitcast.15), kind=kOutput, calls=%fused_computation.15 | convolution fusion | flops 4294967296 | bytes 18874368 | tf_op jit(solution)/shard_map/isjbkqt,sijkptn->ibqpn/dot_general | solution.py:58
  204.6 1.3 copy-done
  206.1 17.6 %fusion.2 = f32[2,2,256,64,128]{2,4,3,1,0:T(8,128)} fusion(bf16[1,2,64,256,128]{4,3,2,1,0:T(8,128)(2,1)} %param.7, bf16[2,256,1,256]{3,1,0,2:T(8,128)(2,1)S(1)} %fusion.29, bf16[2,256,1,256]{3,1,0,2:T(8,128)(2,1)S(1)} %fusion.28), kind=kOutput, calls=%fused_computation.8 | convolution fusion | flops 4295229440 | bytes 42467328 | tf_op jit(solution)/shard_map/isjbc,ibpn->sijcpn/dot_general | solution.py:65
  223.7 25.1 %fusion.27 = (f32[64,2,1,4,1,16,1,256]{7,5,4,3,0,6,1,2:T(8,128)}, f32[64,2,1,4,1,16,1,256]{7,5,4,3,0,6,1,2:T(8,128)}, f32[64,2,1,4,1,16,1,256]{7,5,4,3,0,6,1,2:T(8,128)}, f32[64,2,1,4,1,16,1,256]{7,5,4,3,0,6,1,2:T(8,128)}) fusion(f32[64,2,1,4,2,16,2,256]{7,5,4,3,0,6,1,2:T(8,128)} %bitcast.117), kind=kLoop, calls=%fused_computation.43 | loop fusion | bytes 67108864 | tf_op jit(solution)/shard_map/slice | solution.py:17
  248.8 18.6 %copy_subtract_fusion = (f32[64,2,1,4,1,16,1,256]{7,5,3,1,0,6,4,2:T(8,128)}, f32[64,2,1,4,1,16,1,256]{7,5,3,1,0,6,4,2:T(8,128)}) fusion(f32[64,2,1,4,1,16,1,256]{7,5,4,3,0,6,1,2:T(8,128)} %get-tuple-element.5, f32[64,2,1,4,1,16,1,256]{7,5,4,3,0,6,1,2:T(8,128)} %get-tuple-element.3, f32[64,2,1,4,1,16,1,256]{7,5,4,3,0,6,1,2:T(8,128)} %get-tuple-element.4, ...), kind=kLoop, calls=%fused_computation.6 | loop fusion | flops 4194304 | bytes 50331648 | tf_op jit(solution)/shard_map/sub | solution.py:18
  267.4 9.1 %fusion.1 = bf16[64,8,2,16,256]{4,3,1,0,2:T(8,128)(2,1)} fusion(f32[64,8,1,16,256]{4,3,1,0,2:T(8,128)} %bitcast.118, f32[64,8,1,16,256]{4,3,1,0,2:T(8,128)} %bitcast.119, f32[64,8]{1,0:T(8,128)S(1)} %copy.102), kind=kLoop, calls=%fused_computation.3 | loop fusion | flops 12582912 | bytes 25167872 | tf_op jit(solution)/shard_map/convert_element_type | solution.py:72
  276.5 7.7 %copy.103 = bf16[64,8,2,16,256]{4,3,1,2,0:T(8,128)(2,1)} copy(bf16[64,8,2,16,256]{4,3,1,0,2:T(8,128)(2,1)} %fusion.1) | data formatting | bytes 16777216 | tf_op jit(solution)/shard_map/convert_element_type | solution.py:72
  284.2 15.4 %all-to-all-start.2 = ((bf16[64,8,2,16,256]{4,3,1,2,0:T(8,128)(2,1)}), bf16[64,8,2,16,256]{4,3,1,2,0:T(8,128)(2,1)}, u32[]{:S(2)}, u32[]{:S(2)}) async-start(bf16[64,8,2,16,256]{4,3,1,2,0:T(8,128)(2,1)} %copy.103), calls=%async_computation.2 | async-start | bytes 16777216 | tf_op jit(solution)/shard_map/all_to_all | solution.py:76
  299.7 12.0 %copy.105 = bf16[1,128,1,256,128]{3,4,1,2,0:T(8,128)(2,1)} copy(bf16[1,128,1,256,128]{4,3,2,1,0:T(8,128)(2,1)} %param.6) | data formatting | bytes 16777216 | tf_op args[1]
  311.6 1.3 fusion.17
  313.8 2.0 pad_maximum_fusion
  315.8 98.1 %all-to-all-done.2 = bf16[64,8,2,16,256]{4,3,1,2,0:T(8,128)(2,1)} async-done(((bf16[64,8,2,16,256]{4,3,1,2,0:T(8,128)(2,1)}), bf16[64,8,2,16,256]{4,3,1,2,0:T(8,128)(2,1)}, u32[]{:S(2)}, u32[]{:S(2)}) %all-to-all-start.2) | async-done | bytes 8388640 | tf_op jit(solution)/shard_map/all_to_all | solution.py:76
  413.9 9.4 %fusion.12 = f32[1,256,2,2,256]{1,4,2,3,0:T(8,128)S(1)} fusion(bf16[64,2,256,4,2,16,1]{2,5,4,3,1,0,6:T(8,128)(2,1)} %bitcast.127, bf16[64,2,4,2,16,256,1]{5,4,2,1,3,0,6:T(8,128)(2,1)} %bitcast.41), kind=kOutput, calls=%fused_computation.20 | convolution fusion | flops 4294967296 | bytes 17825792 | tf_op jit(solution)/shard_map/dijbkqt,dijkptn->jbqpn/dot_general | solution.py:73
  423.7 5.3 %all_to_all.43 = bf16[1,256,2,256]{1,2,0,3:T(2,128)(2,1)S(1)} all-to-all(bf16[1,256,2,256]{1,2,0,3:T(2,128)(2,1)S(1)} %copy.110), channel_id=1, replica_groups=mesh['freq'=2,'tile'=64] {'freq'}, dimensions={3} | all-to-all | bytes 524288 | tf_op jit(solution)/shard_map/all_to_all | solution.py:80
  (21 shorter events, 3.1 us)
Async XLA Ops:
  0.6 9.3 %all-to-all-start = ((bf16[2,256,2,128]{3,2,1,0:T(2,128)(2,1)}), bf16[2,256,2,128]{3,2,1,0:T(2,128)(2,1)S(1)}, u32[]{:S(2)}, u32[]{:S(2)}) async-start(bf16[2,256,2,128]{3,2,1,0:T(2,128)(2,1)} %param.5), calls=%async_computation | async-start | bytes 524288 | tf_op jit(solution)/shard_map/all_to_all | solution.py:34
  7.8 2.1 copy-start.1
  56.1 137.0 %all-to-all-start.1 = ((bf16[64,8,2,16,256]{4,3,2,1,0:T(8,128)(2,1)}), bf16[64,8,2,16,256]{4,3,2,1,0:T(8,128)(2,1)}, u32[]{:S(2)}, u32[]{:S(2)}) async-start(bf16[64,8,2,16,256]{4,3,2,1,0:T(8,128)(2,1)} %fusion), calls=%async_computation.1 | async-start | bytes 16777216 | tf_op jit(solution)/shard_map/all_to_all | solution.py:61
  204.6 1.3 copy-start
  284.2 129.6 %all-to-all-start.2 = ((bf16[64,8,2,16,256]{4,3,1,2,0:T(8,128)(2,1)}), bf16[64,8,2,16,256]{4,3,1,2,0:T(8,128)(2,1)}, u32[]{:S(2)}, u32[]{:S(2)}) async-start(bf16[64,8,2,16,256]{4,3,1,2,0:T(8,128)(2,1)} %copy.103), calls=%async_computation.2 | async-start | bytes 16777216 | tf_op jit(solution)/shard_map/all_to_all | solution.py:76
where the time goes:
time: 431 us; the launch traced here: 430 us
  waiting for transfers between devices  211 us (49%)
  local copies, waits for them, and re-layouts  64 us (15%)
  other arithmetic  62.3 us (14%)
  matrix products  56.1 us (13%)
  starting transfers between devices  30.1 us (7%)
  blocking collectives  5.29 us (1%)
    all_to_all x1, waiting for transfers between devices, per_device(): lax.all_to_all(coded_rows, 'tile', split_axis=0, concat_axis=0, tiled=True)  113 us
    all_to_all x1, waiting for transfers between devices, per_device(): lax.all_to_all(returned, 'tile', split_axis=0, concat_axis=0, tiled=True)  98.1 us
    unnamed x6, local copies, waits for them, and re-layouts  27.4 us
    slice x1, local copies, waits for them, and re-layouts, combine_conj(): real_part = shaped[..., 0, :, 0, :] + shaped[..., 1, :, 1, :]  25.1 us
    add x1, other arithmetic, combine_conj(): real_part = shaped[..., 0, :, 0, :] + shaped[..., 1, :, 1, :]  18.9 us
    sub x1, other arithmetic, combine_conj(): imag_part = shaped[..., 0, :, 1, :] - shaped[..., 1, :, 0, :]  18.6 us
    dot_general x1, matrix products, per_device(): jnp.einsum('mjbc,jbpn->mjcpn', column_bases, wavefield, preferred_element...  17.7 us
    dot_general x1, matrix products, per_device(): jnp.einsum('isjbc,ibpn->sijcpn', row_bases.reshape(MT_DEV, tile_count, NT...  17.6 us
  transfers between devices with their start and end apart: 3, of which 2 were waited for; matrix products, arithmetic and copies ran while one was open for 8% of the time, Pallas kernels for 0%

commit v1 on v0

v1 whole, which is shorter than its diff:
```python
import functools
import jax
import jax.numpy as jnp
from jax import lax
from jax.experimental import pallas as pl
from jax.experimental.pallas import tpu as pltpu
from jax.sharding import PartitionSpec as P

NB = 256
RMAX = 64
NVS = 256
TILES = 64
BLOCKS = RMAX // 16
WIDTH = 2 * RMAX
SLOTS = 5
ROWS = 32 * SLOTS
GROUP = 4
CHUNKS = TILES // GROUP
STRIDE = 27
MESH = pl.DeviceIdType.MESH
BF16 = jnp.bfloat16
F32 = jnp.float32


def offset_of(step):
    mixed = lax.rem((step + 1) * STRIDE, TILES)
    return mixed // 16, lax.rem(mixed // 4, 4), lax.rem(mixed, 4)


def shifted(me, step, sign):
    dy, dx, dz = offset_of(step)
    y, x, z = me // 16, lax.rem(me // 4, 4), lax.rem(me, 4)
    y = lax.rem(y + sign * dy + 4, 4)
    x = lax.rem(x + sign * dx + 4, 4)
    z = lax.rem(z + sign * dz + 4, 4)
    return (y * 4 + x) * 4 + z


def conj_block(products, block):
    top = products[32 * block : 32 * block + 16]
    low = products[32 * block + 16 : 32 * block + 32]
    real = top[:, :NVS] + low[:, NVS:]
    imag = top[:, NVS:] - low[:, :NVS]
    return jnp.concatenate([real, imag], 0)


def pack(products0, products1, rank0, rank1, scale0, scale1):
    slots = []
    for slot in range(SLOTS):
        value = None
        if slot < BLOCKS:
            weight = jnp.where(16 * slot < rank0, scale0, 0.0)
            value = conj_block(products0, slot) * weight
        if slot > 0:
            block = SLOTS - 1 - slot
            weight = jnp.where(16 * block < rank1, scale1, 0.0)
            other = conj_block(products1, block) * weight
            value = other if value is None else value + other
        slots.append(value.astype(BF16))
    return jnp.concatenate(slots, 0)


def unpack(packed, rank0, rank1):
    first, second = [], []
    for slot in range(SLOTS):
        real = packed[32 * slot : 32 * slot + 16]
        imag = packed[32 * slot + 16 : 32 * slot + 32]
        both = jnp.concatenate(
            [jnp.concatenate([real, imag], 1), jnp.concatenate([-imag, real], 1)], 0
        )
        if slot < BLOCKS:
            live = jnp.where(16 * slot < rank0, 1.0, 0.0).astype(BF16)
            first.append(both if slot == 0 else both * live)
        if slot > 0:
            block = SLOTS - 1 - slot
            live = jnp.where(16 * block < rank1, 1.0, 0.0).astype(BF16)
            second.append(both if block == 0 else both * live)
    return jnp.concatenate(first, 0), jnp.concatenate(second[::-1], 0)


def body(
    wave_ref, col_hbm, row_hbm, scale_ref, rank_ref,
    fwd_ref, adj_ref,
    vbuf, ubuf, xs, xmat, ybuf, send1, recv1, send2, recv2, dense, acc, halves, landed,
    vsem, usem, ssem1, rsem1, ssem2, rsem2, xsems,
):
    me = lax.axis_index("tile")
    f = lax.axis_index("freq")
    partner = {"freq": 1 - f}

    def v_copy(step):
        d = shifted(me, step, 1)
        return pltpu.make_async_copy(col_hbm.at[d], vbuf.at[d], vsem.at[step])

    def u_copy(part):
        span = pl.ds(part * 16, 16)
        return pltpu.make_async_copy(
            row_hbm.at[:, span], ubuf.at[:, span], usem.at[part]
        )

    @pl.loop(0, TILES)
    def _(step):
        v_copy(step).start()

    barrier = pltpu.get_barrier_semaphore()
    pl.semaphore_signal(barrier, inc=1, device_id=partner, device_id_type=MESH)

    @pl.loop(0, TILES - 1)
    def _(step):
        pl.semaphore_signal(
            barrier, inc=1, device_id={"tile": shifted(me, step, 1)}, device_id_type=MESH
        )

    pl.semaphore_wait(barrier, TILES)

    x_copy = pltpu.make_async_remote_copy(
        src_ref=wave_ref.at[1 - f], dst_ref=xs, send_sem=xsems.at[0],
        recv_sem=xsems.at[1], device_id=partner, device_id_type=MESH,
    )
    x_copy.start()
    for part in range(4):
        u_copy(part).start()
    x_copy.wait()
    mine, theirs = wave_ref[f], xs[...]
    for p in range(2):
        low = jnp.where(f == 0, mine[p], theirs[p])
        high = jnp.where(f == 0, theirs[p], mine[p])
        xmat[:, p * NVS : p * NVS + 128] = low
        xmat[:, p * NVS + 128 : (p + 1) * NVS] = high

    def transfer(send, recv, ssem, rsem, step):
        return pltpu.make_async_remote_copy(
            src_ref=send.at[step], dst_ref=recv.at[step], send_sem=ssem.at[step],
            recv_sem=rsem.at[step], device_id={"tile": shifted(me, step, 1)},
            device_id_type=MESH,
        )

    def deliver(send, recv, ssem, rsem, chunk, values):
        for k in range(GROUP):
            if k < GROUP - 1:
                send[chunk * GROUP + k] = values[k]
        if GROUP > 0:
            last = chunk * GROUP + GROUP - 1

            @pl.when(chunk < CHUNKS - 1)
            def _():
                send[last] = values[GROUP - 1]

            @pl.when(chunk == CHUNKS - 1)
            def _():
                recv[last] = values[GROUP - 1]

        for k in range(GROUP):
            step = chunk * GROUP + k

            @pl.when(step < TILES - 1)
            def _():
                transfer(send, recv, ssem, rsem, step).start()

    def arrive(send, recv, ssem, rsem, chunk):
        for k in range(GROUP):
            step = chunk * GROUP + k

            @pl.when(step < TILES - 1)
            def _():
                transfer(send, recv, ssem, rsem, step).wait_recv()

    def contract(left, right):
        return lax.dot_general(
            left, right, (((0,), (0,)), ((), ())), preferred_element_type=F32
        )

    @pl.loop(0, CHUNKS)
    def _(chunk):
        ids = [shifted(me, chunk * GROUP + k, 1) for k in range(GROUP)]
        for k in range(GROUP):
            v_copy(chunk * GROUP + k).wait()
        left = jnp.concatenate([vbuf[d, r] for d in ids for r in range(2)], 1)
        products = contract(left, xmat[...])
        values = []
        for k, d in enumerate(ids):
            at = 2 * k * WIDTH
            values.append(
                pack(
                    products[at : at + WIDTH], products[at + WIDTH : at + 2 * WIDTH],
                    rank_ref[2 * d, me], rank_ref[2 * d + 1, me],
                    scale_ref[2 * d, me], scale_ref[2 * d + 1, me],
                )
            )
        deliver(send1, recv1, ssem1, rsem1, chunk, values)

    for part in range(4):
        u_copy(part).wait()

    acc[...] = jnp.zeros_like(acc)

    @pl.loop(0, CHUNKS)
    def _(chunk):
        arrive(send1, recv1, ssem1, rsem1, chunk)
        ids = [shifted(me, chunk * GROUP + k, -1) for k in range(GROUP)]
        for k, j in enumerate(ids):
            first, second = unpack(
                recv1[chunk * GROUP + k], rank_ref[2 * me, j], rank_ref[2 * me + 1, j]
            )
            dense[k * WIDTH : (k + 1) * WIDTH] = first
            dense[(GROUP + k) * WIDTH : (GROUP + k + 1) * WIDTH] = second
        for r in range(2):
            left = jnp.concatenate([ubuf[r, j] for j in ids], 1)
            right = dense[r * GROUP * WIDTH : (r + 1) * GROUP * WIDTH]
            acc[r] += jnp.dot(left, right, preferred_element_type=F32)

    for r in range(2):
        ybuf[r] = acc[r].astype(BF16)

    @pl.loop(0, CHUNKS)
    def _(chunk):
        ids = [shifted(me, chunk * GROUP + k, 1) for k in range(GROUP)]
        products = [
            contract(jnp.concatenate([ubuf[r, j] for j in ids], 1), ybuf[r])
            for r in range(2)
        ]
        values = []
        for k, j in enumerate(ids):
            at = k * WIDTH
            values.append(
                pack(
                    products[0][at : at + WIDTH], products[1][at : at + WIDTH],
                    rank_ref[2 * me, j], rank_ref[2 * me + 1, j],
                    scale_ref[2 * me, j], scale_ref[2 * me + 1, j],
                )
            )
        deliver(send2, recv2, ssem2, rsem2, chunk, values)

    for r in range(2):
        for p in range(2):
            fwd_ref[r, p] = ybuf[r, :, p * NVS : (p + 1) * NVS]
    acc[0] = jnp.zeros((NB, 2 * NVS), F32)

    @pl.loop(0, CHUNKS)
    def _(chunk):
        arrive(send2, recv2, ssem2, rsem2, chunk)
        ids = [shifted(me, chunk * GROUP + k, -1) for k in range(GROUP)]
        for k, d in enumerate(ids):
            first, second = unpack(
                recv2[chunk * GROUP + k], rank_ref[2 * d, me], rank_ref[2 * d + 1, me]
            )
            dense[2 * k * WIDTH : (2 * k + 1) * WIDTH] = first
            dense[(2 * k + 1) * WIDTH : (2 * k + 2) * WIDTH] = second
        left = jnp.concatenate([vbuf[d, r] for d in ids for r in range(2)], 1)
        acc[0] += jnp.dot(left, dense[...], preferred_element_type=F32)

    for half in range(2):
        for p in range(2):
            at = p * NVS + half * 128
            halves[half, p] = acc[0, :, at : at + 128].astype(BF16)
    out_copy = pltpu.make_async_remote_copy(
        src_ref=halves.at[1 - f], dst_ref=landed, send_sem=xsems.at[2],
        recv_sem=xsems.at[3], device_id=partner, device_id_type=MESH,
    )
    out_copy.start()
    adj_ref[f] = halves[f]

    @pl.loop(0, TILES - 1)
    def _(step):
        transfer(send1, recv1, ssem1, rsem1, step).wait_send()
        transfer(send2, recv2, ssem2, rsem2, step).wait_send()

    out_copy.wait()
    adj_ref[1 - f] = landed[...]


def per_device(wave_in, column_basis, row_basis, tile_scale, tile_ranks):
    wave = jnp.transpose(wave_in, (0, 2, 1, 3))
    columns = column_basis.reshape(TILES, 2, NB, WIDTH)
    rows = row_basis.reshape(2, TILES, NB, WIDTH)
    anywhere = pl.BlockSpec(memory_space=pl.ANY)
    vmem = pl.BlockSpec(memory_space=pltpu.VMEM)
    smem = pl.BlockSpec(memory_space=pltpu.SMEM)
    packed = pltpu.VMEM((TILES, ROWS, NVS), BF16)
    forward, adjoint = pl.pallas_call(
        body,
        out_shape=(
            jax.ShapeDtypeStruct((2, 2, NB, NVS), BF16),
            jax.ShapeDtypeStruct((2, 2, NB, 128), BF16),
        ),
        in_specs=[vmem, anywhere, anywhere, smem, smem],
        out_specs=(vmem, vmem),
        scratch_shapes=[
            pltpu.VMEM((TILES, 2, NB, WIDTH), BF16),
            pltpu.VMEM((2, TILES, NB, WIDTH), BF16),
            pltpu.VMEM((2, NB, 128), BF16),
            pltpu.VMEM((NB, 2 * NVS), BF16),
            pltpu.VMEM((2, NB, 2 * NVS), BF16),
            packed, packed, packed, packed,
            pltpu.VMEM((2 * GROUP * WIDTH, 2 * NVS), BF16),
            pltpu.VMEM((2, NB, 2 * NVS), F32),
            pltpu.VMEM((2, 2, NB, 128), BF16),
            pltpu.VMEM((2, NB, 128), BF16),
            pltpu.SemaphoreType.DMA((TILES,)),
            pltpu.SemaphoreType.DMA((4,)),
            pltpu.SemaphoreType.DMA((TILES,)),
            pltpu.SemaphoreType.DMA((TILES,)),
            pltpu.SemaphoreType.DMA((TILES,)),
            pltpu.SemaphoreType.DMA((TILES,)),
            pltpu.SemaphoreType.DMA((4,)),
        ],
        compiler_params=pltpu.CompilerParams(
            collective_id=0, has_side_effects=True, vmem_limit_bytes=63 << 20
        ),
        name="normal_operator",
    )(wave, columns, rows, tile_scale[0], tile_ranks[0])
    forward_out = jnp.transpose(forward, (0, 2, 1, 3)).reshape(1, 2 * NB, 2, NVS)
    adjoint_out = jnp.transpose(adjoint, (0, 2, 1, 3))
    return forward_out, adjoint_out


def solution(mesh):
    return jax.shard_map(
        per_device,
        mesh=mesh,
        in_specs=(
            P(None, "tile", None, "freq"),
            P("freq", None, "tile", None, None),
            P("freq", "tile", None, None, None),
            P("freq", None, None),
            P("freq", None, None),
        ),
        out_specs=(P("freq", "tile", None, None), P(None, "tile", None, "freq")),
        check_vma=False,
    )
```

time: 431 us -> 177 us (0.41)
  the two profiles are of different devices: /device:TPU:51 before, /device:TPU:1 now
where the time goes in v1:
time: 177 us; the launch traced here: 176 us
  Pallas kernels  167 us (94%)
  local copies, waits for them, and re-layouts  8.99 us (5%)
    pallas_call x1, Pallas kernels, per_device(): pl.pallas_call(body, out_shape=(jax.ShapeDtypeStruct((2, 2, NB, NVS), BF1...  167 us
    unnamed x5, local copies, waits for them, and re-layouts  7.91 us

profile of v1, /device:TPU:1, one launch (start us, length us, event | category | flops | bytes accessed | tf_op | source)
XLA Modules:
  0.0 176.5 jit_solution(9591353686040569432)
XLA Ops:
  0.6 1.5 copy.12
  2.1 1.5 copy.13
  3.6 1.7 copy.18
  5.3 166.9 %normal_operator.1 = (bf16[2,2,256,256]{3,2,1,0:T(8,128)(2,1)}, bf16[2,2,256,128]{3,2,1,0:T(8,128)(2,1)}) custom-call(bf16[2,2,256,128]{3,2,1,0:T(8,128)(2,1)} %bitcast.13, bf16[64,2,256,128]{3,2,1,0:T(8,128)(2,1)} %bitcast.10, bf16[2,64,256,128]{3,2,1,0:T(8,128)(2,1)} %bitcast.11, f32[128,64]{1,0:T(8,128)} %bitcast.15, s32[128,64]{1,0:T(8,128)} %bitcast.16), custom_call_target="tpu_custom_call" | custom-call | tf_op jit(solution)/shard_map/normal_operator/pallas_call | solution.py:280
  172.2 1.1 copy.14
  173.2 1.3 copy.15
  174.6 1.9 %copy.16 = bf16[2,256,2,128]{3,2,1,0:T(2,128)(2,1)} copy(bf16[2,256,2,128]{3,1,2,0:T(8,128)(2,1)} %bitcast.17) | data formatting | bytes 524288

commit v2 on v1

v2 whole, which is shorter than its diff:
```python
import functools
import jax
import jax.numpy as jnp
from jax import lax
from jax.experimental import pallas as pl
from jax.experimental.pallas import tpu as pltpu
from jax.sharding import PartitionSpec as P

NB = 256
RMAX = 64
NVS = 256
TILES = 64
HALF = NVS // 2
BLOCKS = RMAX // 16
WIDTH = 2 * RMAX
SLOTS = 5
ROWS = 32 * SLOTS
GROUP = 4
CHUNKS = TILES // GROUP
STRIDE = 27
MESH = pl.DeviceIdType.MESH
BF16 = jnp.bfloat16
F32 = jnp.float32


def offset_of(step):
    mixed = lax.rem((step + 1) * STRIDE, TILES)
    return mixed // 16, lax.rem(mixed // 4, 4), lax.rem(mixed, 4)


def shifted(me, step, sign):
    dy, dx, dz = offset_of(step)
    y, x, z = me // 16, lax.rem(me // 4, 4), lax.rem(me, 4)
    y = lax.rem(y + sign * dy + 4, 4)
    x = lax.rem(x + sign * dx + 4, 4)
    z = lax.rem(z + sign * dz + 4, 4)
    return (y * 4 + x) * 4 + z


def conj_block(products, block):
    top = products[32 * block : 32 * block + 16]
    low = products[32 * block + 16 : 32 * block + 32]
    real = top[:, :HALF] + low[:, HALF:]
    imag = top[:, HALF:] - low[:, :HALF]
    return jnp.concatenate([real, imag], 0)


def pack(products0, products1, rank0, rank1, scale0, scale1):
    slots = []
    for slot in range(SLOTS):
        value = None
        if slot < BLOCKS:
            weight = jnp.where(16 * slot < rank0, scale0, 0.0)
            value = conj_block(products0, slot) * weight
        if slot > 0:
            block = SLOTS - 1 - slot
            weight = jnp.where(16 * block < rank1, scale1, 0.0)
            other = conj_block(products1, block) * weight
            value = other if value is None else value + other
        slots.append(value.astype(BF16))
    return jnp.concatenate(slots, 0)


def unpack(packed, rank0, rank1):
    first, second = [], []
    for slot in range(SLOTS):
        real = packed[32 * slot : 32 * slot + 16]
        imag = packed[32 * slot + 16 : 32 * slot + 32]
        both = jnp.concatenate(
            [jnp.concatenate([real, imag], 1), jnp.concatenate([-imag, real], 1)], 0
        )
        if slot < BLOCKS:
            live = jnp.where(16 * slot < rank0, 1.0, 0.0).astype(BF16)
            first.append(both if slot == 0 else both * live)
        if slot > 0:
            block = SLOTS - 1 - slot
            live = jnp.where(16 * block < rank1, 1.0, 0.0).astype(BF16)
            second.append(both if block == 0 else both * live)
    return jnp.concatenate(first, 0), jnp.concatenate(second[::-1], 0)


def body(
    wave_ref, col_hbm, row_hbm, scale_ref, rank_ref,
    fwd_ref, adj_ref,
    vbuf, ubuf, landing, xmat, ybuf, send, recv, dense, acc, leaving, landed,
    vsem, usem, ssem, rsem, xsems,
):
    me = lax.axis_index("tile")
    f = lax.axis_index("freq")
    partner = {"freq": 1 - f}
    last = TILES - 1

    def v_copy(step, d):
        return pltpu.make_async_copy(col_hbm.at[d], vbuf.at[d], vsem.at[step])

    def u_copy(part):
        span = pl.ds(part * 16, 16)
        return pltpu.make_async_copy(
            row_hbm.at[:, span], ubuf.at[:, span], usem.at[part]
        )

    barrier = pltpu.get_barrier_semaphore()
    pl.semaphore_signal(barrier, inc=1, device_id=partner, device_id_type=MESH)
    ys = [16 * lax.rem(me // 16 + k, 4) for k in range(4)]
    xs = [4 * lax.rem(me // 4 + k, 4) for k in range(4)]
    zs = [lax.rem(me + k, 4) for k in range(4)]
    for step in range(TILES):
        mixed = (step + 1) * STRIDE % TILES
        d = ys[mixed // 16] + xs[mixed // 4 % 4] + zs[mixed % 4]
        if step < last:
            pl.semaphore_signal(
                barrier, inc=1, device_id={"tile": d}, device_id_type=MESH
            )
        v_copy(step, d).start()
    for part in range(4):
        u_copy(part).start()

    def targets(chunk, sign):
        return [shifted(me, chunk * GROUP + k, sign) for k in range(GROUP)]

    def transfer(phase, step):
        return pltpu.make_async_remote_copy(
            src_ref=send.at[phase, step], dst_ref=recv.at[phase, step],
            send_sem=ssem.at[phase, step], recv_sem=rsem.at[phase, step],
            device_id={"tile": shifted(me, step, 1)}, device_id_type=MESH,
        )

    def store(phase, chunk, values):
        for k in range(GROUP):
            send[phase, chunk * GROUP + k] = values[k]

        @pl.when(chunk == CHUNKS - 1)
        def _():
            recv[phase, last] = values[GROUP - 1]

    def depart(phase, chunk):
        for k in range(GROUP - 1):
            transfer(phase, chunk * GROUP + k).start()

        @pl.when(chunk < CHUNKS - 1)
        def _():
            transfer(phase, chunk * GROUP + GROUP - 1).start()

    def arrive(phase, chunk):
        for k in range(GROUP - 1):
            transfer(phase, chunk * GROUP + k).wait_recv()

        @pl.when(chunk < CHUNKS - 1)
        def _():
            transfer(phase, chunk * GROUP + GROUP - 1).wait_recv()

    def sent(phase):
        @pl.loop(0, last)
        def _(step):
            transfer(phase, step).wait_send()

    def contract(left, right):
        return lax.dot_general(
            left, right, (((0,), (0,)), ((), ())), preferred_element_type=F32
        )

    def code(half, chunk):
        ids = targets(chunk, 1)
        left = jnp.concatenate([vbuf[d, r] for d in ids for r in range(2)], 1)
        products = contract(left, xmat[half])
        values = []
        for k, d in enumerate(ids):
            at = 2 * k * WIDTH
            values.append(
                pack(
                    products[at : at + WIDTH], products[at + WIDTH : at + 2 * WIDTH],
                    rank_ref[me, 2 * d], rank_ref[me, 2 * d + 1],
                    scale_ref[me, 2 * d], scale_ref[me, 2 * d + 1],
                )
            )
        store(half, chunk, values)

    def loaded(chunk):
        for k in range(GROUP):
            v_copy(chunk * GROUP + k, 0).wait()

    def expand(half):
        acc[...] = jnp.zeros_like(acc)

        @pl.loop(0, CHUNKS)
        def _(chunk):
            arrive(half, chunk)
            ids = targets(chunk, -1)
            for k, j in enumerate(ids):
                first, second = unpack(
                    recv[half, chunk * GROUP + k],
                    rank_ref[j, 2 * me], rank_ref[j, 2 * me + 1],
                )
                dense[k * WIDTH : (k + 1) * WIDTH] = first
                dense[(GROUP + k) * WIDTH : (GROUP + k + 1) * WIDTH] = second
            for r in range(2):
                left = jnp.concatenate([ubuf[r, j] for j in ids], 1)
                right = dense[r * GROUP * WIDTH : (r + 1) * GROUP * WIDTH]
                acc[r] += jnp.dot(left, right, preferred_element_type=F32)

        for r in range(2):
            ybuf[half, r] = acc[r].astype(BF16)

    def code_back(half):
        @pl.loop(0, CHUNKS)
        def _(chunk):
            ids = targets(chunk, 1)
            products = [
                contract(
                    jnp.concatenate([ubuf[r, j] for j in ids], 1), ybuf[half, r]
                )
                for r in range(2)
            ]
            values = []
            for k, j in enumerate(ids):
                at = k * WIDTH
                values.append(
                    pack(
                        products[0][at : at + WIDTH], products[1][at : at + WIDTH],
                        rank_ref[j, 2 * me], rank_ref[j, 2 * me + 1],
                        scale_ref[j, 2 * me], scale_ref[j, 2 * me + 1],
                    )
                )
            store(2 + half, chunk, values)
            depart(2 + half, chunk)

    def expand_back(half):
        acc[0] = jnp.zeros((NB, NVS), F32)

        @pl.loop(0, CHUNKS)
        def _(chunk):
            arrive(2 + half, chunk)
            ids = targets(chunk, -1)
            for k, d in enumerate(ids):
                first, second = unpack(
                    recv[2 + half, chunk * GROUP + k],
                    rank_ref[me, 2 * d], rank_ref[me, 2 * d + 1],
                )
                dense[2 * k * WIDTH : (2 * k + 1) * WIDTH] = first
                dense[(2 * k + 1) * WIDTH : (2 * k + 2) * WIDTH] = second
            left = jnp.concatenate([vbuf[d, r] for d in ids for r in range(2)], 1)
            acc[0] += jnp.dot(left, dense[...], preferred_element_type=F32)

    for p in range(2):
        xmat[0, :, p * HALF : (p + 1) * HALF] = wave_ref[f, p]
    loaded(0)
    code(0, 0)
    pl.semaphore_wait(barrier, TILES)
    depart(0, 0)
    x_copy = pltpu.make_async_remote_copy(
        src_ref=wave_ref.at[1 - f], dst_ref=landing, send_sem=xsems.at[0],
        recv_sem=xsems.at[1], device_id=partner, device_id_type=MESH,
    )
    x_copy.start()

    @pl.loop(1, CHUNKS)
    def _(chunk):
        loaded(chunk)
        code(0, chunk)
        depart(0, chunk)

    x_copy.wait()
    for p in range(2):
        xmat[1, :, p * HALF : (p + 1) * HALF] = landing[p]

    @pl.loop(0, CHUNKS)
    def _(chunk):
        code(1, chunk)
        depart(1, chunk)

    for part in range(4):
        u_copy(part).wait()
    expand(0)
    code_back(0)
    expand(1)
    code_back(1)
    for r in range(2):
        for p in range(2):
            own = ybuf[0, r, :, p * HALF : (p + 1) * HALF]
            other = ybuf[1, r, :, p * HALF : (p + 1) * HALF]
            rows = slice(r * NB, (r + 1) * NB)
            fwd_ref[p, rows, :HALF] = jnp.where(f == 0, own, other)
            fwd_ref[p, rows, HALF:] = jnp.where(f == 0, other, own)
    sent(0)
    sent(1)
    expand_back(0)
    for p in range(2):
        adj_ref[f, p] = acc[0, :, p * HALF : (p + 1) * HALF].astype(BF16)
    expand_back(1)
    for p in range(2):
        leaving[p] = acc[0, :, p * HALF : (p + 1) * HALF].astype(BF16)
    out_copy = pltpu.make_async_remote_copy(
        src_ref=leaving, dst_ref=landed, send_sem=xsems.at[2],
        recv_sem=xsems.at[3], device_id=partner, device_id_type=MESH,
    )
    out_copy.start()
    sent(2)
    sent(3)
    out_copy.wait()
    adj_ref[1 - f] = landed[...]


def per_device(wave_in, column_basis, row_basis, tile_scale, tile_ranks):
    wave = jnp.transpose(wave_in, (0, 2, 1, 3))
    columns = column_basis.reshape(TILES, 2, NB, WIDTH)
    rows = row_basis.reshape(2, TILES, NB, WIDTH)
    anywhere = pl.BlockSpec(memory_space=pl.ANY)
    vmem = pl.BlockSpec(memory_space=pltpu.VMEM)
    smem = pl.BlockSpec(memory_space=pltpu.SMEM)
    packed = pltpu.VMEM((4, TILES, ROWS, HALF), BF16)
    forward, adjoint = pl.pallas_call(
        body,
        out_shape=(
            jax.ShapeDtypeStruct((2, 2 * NB, NVS), BF16),
            jax.ShapeDtypeStruct((2, 2, NB, HALF), BF16),
        ),
        in_specs=[vmem, anywhere, anywhere, smem, smem],
        out_specs=(vmem, vmem),
        scratch_shapes=[
            pltpu.VMEM((TILES, 2, NB, WIDTH), BF16),
            pltpu.VMEM((2, TILES, NB, WIDTH), BF16),
            pltpu.VMEM((2, NB, HALF), BF16),
            pltpu.VMEM((2, NB, NVS), BF16),
            pltpu.VMEM((2, 2, NB, NVS), BF16),
            packed, packed,
            pltpu.VMEM((2 * GROUP * WIDTH, NVS), BF16),
            pltpu.VMEM((2, NB, NVS), F32),
            pltpu.VMEM((2, NB, HALF), BF16),
            pltpu.VMEM((2, NB, HALF), BF16),
            pltpu.SemaphoreType.DMA((TILES,)),
            pltpu.SemaphoreType.DMA((4,)),
            pltpu.SemaphoreType.DMA((4, TILES)),
            pltpu.SemaphoreType.DMA((4, TILES)),
            pltpu.SemaphoreType.DMA((4,)),
        ],
        compiler_params=pltpu.CompilerParams(
            collective_id=0, has_side_effects=True, vmem_limit_bytes=63 << 20
        ),
        name="normal_operator",
    )(wave, columns, rows, tile_scale[0].T, tile_ranks[0].T)
    forward_out = jnp.transpose(forward, (1, 0, 2))[None]
    adjoint_out = jnp.transpose(adjoint, (0, 2, 1, 3))
    return forward_out, adjoint_out


def solution(mesh):
    return jax.shard_map(
        per_device,
        mesh=mesh,
        in_specs=(
            P(None, "tile", None, "freq"),
            P("freq", None, "tile", None, None),
            P("freq", "tile", None, None, None),
            P("freq", None, None),
            P("freq", None, None),
        ),
        out_specs=(P("freq", "tile", None, None), P(None, "tile", None, "freq")),
        check_vma=False,
    )
```

time: 177 us -> 143 us (0.81)
  Pallas kernels: 167 us -> 136 us
  local copies, waits for them, and re-layouts: 8.99 us -> 5.98 us
    pallas_call x1, Pallas kernels: 167 us -> 136 us  [per_device(): pl.pallas_call(body, out_shape=(jax.ShapeDtypeStruct((2, 2 * NB, NVS), BF...]
    unnamed x5 -> x3, local copies, waits for them, and re-layouts: 7.91 us -> 5.98 us
where the time goes in v2:
time: 143 us
  Pallas kernels  136 us (95%)
  local copies, waits for them, and re-layouts  5.98 us (4%)
    pallas_call x1, Pallas kernels, per_device(): pl.pallas_call(body, out_shape=(jax.ShapeDtypeStruct((2, 2 * NB, NVS), BF...  136 us
    unnamed x3, local copies, waits for them, and re-layouts  5.98 us

profile of v2, /device:TPU:1, one launch (start us, length us, event | category | flops | bytes accessed | tf_op | source)
XLA Modules:
  0.0 143.0 jit_solution(11211421526972390659)
XLA Ops:
  0.6 1.7 %copy.11 = bf16[2,256,2,128]{3,1,2,0:T(8,128)(2,1)} copy(bf16[2,256,2,128]{3,2,1,0:T(2,128)(2,1)} %param.5) | data formatting | bytes 524288 | tf_op args[0]
  2.3 136.4 %normal_operator.1 = (bf16[2,512,256]{2,1,0:T(8,128)(2,1)}, bf16[2,2,256,128]{3,2,1,0:T(8,128)(2,1)}) custom-call(bf16[2,2,256,128]{3,2,1,0:T(8,128)(2,1)} %bitcast.17, bf16[64,2,256,128]{3,2,1,0:T(8,128)(2,1)} %bitcast.15, bf16[2,64,256,128]{3,2,1,0:T(8,128)(2,1)} %bitcast.16, f32[64,128]{1,0:T(8,128)} %bitcast.20, s32[64,128]{1,0:T(8,128)} %bitcast.21), custom_call_target="tpu_custom_call" | custom-call | tf_op jit(solution)/shard_map/normal_operator/pallas_call | solution.py:311
  138.7 2.4 %copy.8 = bf16[1,512,2,256]{3,2,1,0:T(2,128)(2,1)} copy(bf16[1,512,2,256]{3,1,2,0:T(8,128)(2,1)} %bitcast.18) | data formatting | bytes 1048576
  141.1 1.9 %copy.9 = bf16[2,256,2,128]{3,2,1,0:T(2,128)(2,1)} copy(bf16[2,256,2,128]{3,1,2,0:T(8,128)(2,1)} %bitcast.19) | data formatting | bytes 524288

commit v3 on v2

--- a/solution.py
+++ b/solution.py
@@ -17,7 +17,7 @@
 ROWS = 32 * SLOTS
 GROUP = 4
 CHUNKS = TILES // GROUP
-STRIDE = 27
+STRIDE = 5
 MESH = pl.DeviceIdType.MESH
 BF16 = jnp.bfloat16
 F32 = jnp.float32
@@ -80,10 +80,11 @@
 
 
 def body(
-    wave_ref, col_hbm, row_hbm, scale_ref, rank_ref,
-    fwd_ref, adj_ref,
-    vbuf, ubuf, landing, xmat, ybuf, send, recv, dense, acc, leaving, landed,
-    vsem, usem, ssem, rsem, xsems,
+    wave_hbm, col_hbm, row_hbm, scale_hbm, rank_hbm,
+    fwd_hbm, adj_hbm,
+    scale_ref, rank_ref, vbuf, ubuf, waves, xmat, ybuf, send, recv, dense, acc,
+    stripes, fwdbuf, staying, leaving,
+    vsem, usem, ssem, rsem, xsems, lsems,
 ):
     me = lax.axis_index("tile")
     f = lax.axis_index("freq")
@@ -99,19 +100,31 @@
             row_hbm.at[:, span], ubuf.at[:, span], usem.at[part]
         )
 
+    def own_rows(index):
+        return pl.ds(pl.multiple_of(index * 2 * NB, 2 * NB), 2 * NB)
+
     barrier = pltpu.get_barrier_semaphore()
-    pl.semaphore_signal(barrier, inc=1, device_id=partner, device_id_type=MESH)
     ys = [16 * lax.rem(me // 16 + k, 4) for k in range(4)]
     xs = [4 * lax.rem(me // 4 + k, 4) for k in range(4)]
     zs = [lax.rem(me + k, 4) for k in range(4)]
+    order = [(step + 1) * STRIDE % TILES for step in range(TILES)]
+    ids = [ys[at // 16] + xs[at // 4 % 4] + zs[at % 4] for at in order]
+    hops = [min(at // 16, 1) + min(at // 4 % 4, 1) + min(at % 4, 1)
+            + (at // 16 == 2) + (at // 4 % 4 == 2) + (at % 4 == 2) for at in order]
+    for step in sorted(range(last), key=lambda step: -hops[step]):
+        pl.semaphore_signal(
+            barrier, inc=1, device_id={"tile": ids[step]}, device_id_type=MESH
+        )
+    pl.semaphore_signal(barrier, inc=1, device_id=partner, device_id_type=MESH)
+    table_copies = [
+        pltpu.make_async_copy(scale_hbm, scale_ref, lsems.at[0]),
+        pltpu.make_async_copy(rank_hbm, rank_ref, lsems.at[1]),
+        pltpu.make_async_copy(wave_hbm.at[own_rows(f)], waves.at[0], lsems.at[2]),
+    ]
+    for copy in table_copies:
+        copy.start()
     for step in range(TILES):
-        mixed = (step + 1) * STRIDE % TILES
-        d = ys[mixed // 16] + xs[mixed // 4 % 4] + zs[mixed % 4]
-        if step < last:
-            pl.semaphore_signal(
-                barrier, inc=1, device_id={"tile": d}, device_id_type=MESH
-            )
-        v_copy(step, d).start()
+        v_copy(step, ids[step]).start()
     for part in range(4):
         u_copy(part).start()
 
@@ -241,14 +254,26 @@
             left = jnp.concatenate([vbuf[d, r] for d in ids for r in range(2)], 1)
             acc[0] += jnp.dot(left, dense[...], preferred_element_type=F32)
 
-    for p in range(2):
-        xmat[0, :, p * HALF : (p + 1) * HALF] = wave_ref[f, p]
+    def split(half):
+        stripes[: 2 * NB] = waves[half].astype(F32)
+        for p in range(2):
+            part = stripes[pl.ds(p, NB, stride=2), :]
+            xmat[half, :, p * HALF : (p + 1) * HALF] = part.astype(BF16)
+
+    def merge(target):
+        for p in range(2):
+            stripes[pl.ds(p, NB, stride=2), :] = acc[0, :, p * HALF : (p + 1) * HALF]
+        target[...] = stripes[: 2 * NB].astype(BF16)
+
+    for copy in table_copies:
+        copy.wait()
+    split(0)
     loaded(0)
     code(0, 0)
     pl.semaphore_wait(barrier, TILES)
     depart(0, 0)
     x_copy = pltpu.make_async_remote_copy(
-        src_ref=wave_ref.at[1 - f], dst_ref=landing, send_sem=xsems.at[0],
+        src_ref=wave_hbm.at[own_rows(1 - f)], dst_ref=waves.at[1], send_sem=xsems.at[0],
         recv_sem=xsems.at[1], device_id=partner, device_id_type=MESH,
     )
     x_copy.start()
@@ -260,8 +285,7 @@
         depart(0, chunk)
 
     x_copy.wait()
-    for p in range(2):
-        xmat[1, :, p * HALF : (p + 1) * HALF] = landing[p]
+    split(1)
 
     @pl.loop(0, CHUNKS)
     def _(chunk):
@@ -276,70 +300,78 @@
     code_back(1)
     for r in range(2):
         for p in range(2):
-            own = ybuf[0, r, :, p * HALF : (p + 1) * HALF]
-            other = ybuf[1, r, :, p * HALF : (p + 1) * HALF]
-            rows = slice(r * NB, (r + 1) * NB)
-            fwd_ref[p, rows, :HALF] = jnp.where(f == 0, own, other)
-            fwd_ref[p, rows, HALF:] = jnp.where(f == 0, other, own)
+            own = ybuf[0, r, :, p * HALF : (p + 1) * HALF].astype(F32)
+            other = ybuf[1, r, :, p * HALF : (p + 1) * HALF].astype(F32)
+            at = 4 * NB * r + p
+            stripes[pl.ds(at, NB, stride=4), :] = jnp.where(f == 0, own, other)
+            stripes[pl.ds(at + 2, NB, stride=4), :] = jnp.where(f == 0, other, own)
+    fwdbuf[...] = stripes[...].astype(BF16)
+    fwd_copy = pltpu.make_async_copy(fwdbuf, fwd_hbm, lsems.at[3])
+    fwd_copy.start()
     sent(0)
     sent(1)
     expand_back(0)
-    for p in range(2):
-        adj_ref[f, p] = acc[0, :, p * HALF : (p + 1) * HALF].astype(BF16)
+    merge(staying)
+    adj_copy = pltpu.make_async_copy(staying, adj_hbm.at[own_rows(f)], lsems.at[4])
+    adj_copy.start()
     expand_back(1)
-    for p in range(2):
-        leaving[p] = acc[0, :, p * HALF : (p + 1) * HALF].astype(BF16)
+    merge(leaving)
     out_copy = pltpu.make_async_remote_copy(
-        src_ref=leaving, dst_ref=landed, send_sem=xsems.at[2],
+        src_ref=leaving, dst_ref=adj_hbm.at[own_rows(f)], send_sem=xsems.at[2],
         recv_sem=xsems.at[3], device_id=partner, device_id_type=MESH,
     )
     out_copy.start()
     sent(2)
     sent(3)
+    fwd_copy.wait()
+    adj_copy.wait()
     out_copy.wait()
-    adj_ref[1 - f] = landed[...]
 
 
 def per_device(wave_in, column_basis, row_basis, tile_scale, tile_ranks):
-    wave = jnp.transpose(wave_in, (0, 2, 1, 3))
+    wave = wave_in.reshape(4 * NB, HALF)
     columns = column_basis.reshape(TILES, 2, NB, WIDTH)
     rows = row_basis.reshape(2, TILES, NB, WIDTH)
     anywhere = pl.BlockSpec(memory_space=pl.ANY)
-    vmem = pl.BlockSpec(memory_space=pltpu.VMEM)
-    smem = pl.BlockSpec(memory_space=pltpu.SMEM)
     packed = pltpu.VMEM((4, TILES, ROWS, HALF), BF16)
     forward, adjoint = pl.pallas_call(
         body,
         out_shape=(
-            jax.ShapeDtypeStruct((2, 2 * NB, NVS), BF16),
-            jax.ShapeDtypeStruct((2, 2, NB, HALF), BF16),
+            jax.ShapeDtypeStruct((8 * NB, HALF), BF16),
+            jax.ShapeDtypeStruct((4 * NB, HALF), BF16),
         ),
-        in_specs=[vmem, anywhere, anywhere, smem, smem],
-        out_specs=(vmem, vmem),
+        in_specs=[anywhere] * 5,
+        out_specs=(anywhere, anywhere),
         scratch_shapes=[
+            pltpu.SMEM((TILES, 2 * TILES), F32),
+            pltpu.SMEM((TILES, 2 * TILES), jnp.int32),
             pltpu.VMEM((TILES, 2, NB, WIDTH), BF16),
             pltpu.VMEM((2, TILES, NB, WIDTH), BF16),
-            pltpu.VMEM((2, NB, HALF), BF16),
+            pltpu.VMEM((2, 2 * NB, HALF), BF16),
             pltpu.VMEM((2, NB, NVS), BF16),
             pltpu.VMEM((2, 2, NB, NVS), BF16),
             packed, packed,
             pltpu.VMEM((2 * GROUP * WIDTH, NVS), BF16),
             pltpu.VMEM((2, NB, NVS), F32),
-            pltpu.VMEM((2, NB, HALF), BF16),
-            pltpu.VMEM((2, NB, HALF), BF16),
+            pltpu.VMEM((8 * NB, HALF), F32),
+            pltpu.VMEM((8 * NB, HALF), BF16),
+            pltpu.VMEM((2 * NB, HALF), BF16),
+            pltpu.VMEM((2 * NB, HALF), BF16),
             pltpu.SemaphoreType.DMA((TILES,)),
             pltpu.SemaphoreType.DMA((4,)),
             pltpu.SemaphoreType.DMA((4, TILES)),
             pltpu.SemaphoreType.DMA((4, TILES)),
             pltpu.SemaphoreType.DMA((4,)),
+            pltpu.SemaphoreType.DMA((5,)),
         ],
         compiler_params=pltpu.CompilerParams(
-            collective_id=0, has_side_effects=True, vmem_limit_bytes=63 << 20
+            collective_id=0, has_side_effects=True, vmem_limit_bytes=56 << 20
         ),
         name="normal_operator",
     )(wave, columns, rows, tile_scale[0].T, tile_ranks[0].T)
-    forward_out = jnp.transpose(forward, (1, 0, 2))[None]
-    adjoint_out = jnp.transpose(adjoint, (0, 2, 1, 3))
+    forward = forward.reshape(2 * NB, 2, 2, HALF).transpose(0, 2, 1, 3)
+    forward_out = forward.reshape(1, 2 * NB, 2, NVS)
+    adjoint_out = adjoint.reshape(2, NB, 2, HALF)
     return forward_out, adjoint_out
 
 

time: 143 us -> 143 us (level); the launches traced: 143 us -> 141 us
  local copies, waits for them, and re-layouts: 5.98 us -> 4.03 us
    unnamed x3 -> x2, local copies, waits for them, and re-layouts: 5.98 us -> 4.03 us
where the time goes in v3:
time: 143 us; the launch traced here: 141 us
  Pallas kernels  137 us (96%)
  local copies, waits for them, and re-layouts  4.03 us (3%)
    pallas_call x1, Pallas kernels, per_device(): pl.pallas_call(body, out_shape=(jax.ShapeDtypeStruct((8 * NB, HALF), BF16...  137 us
    unnamed x2, local copies, waits for them, and re-layouts  4.03 us

profile of v3, /device:TPU:1, one launch (start us, length us, event | category | flops | bytes accessed | tf_op | source)
XLA Modules:
  0.0 141.4 jit_solution(545546011868358702)
XLA Ops:
  0.6 136.7 %normal_operator.1 = (bf16[2048,128]{1,0:T(8,128)(2,1)}, bf16[1024,128]{1,0:T(8,128)(2,1)}) custom-call(bf16[1024,128]{1,0:T(8,128)(2,1)} %bitcast.18, bf16[64,2,256,128]{3,2,1,0:T(8,128)(2,1)} %bitcast.15, bf16[2,64,256,128]{3,2,1,0:T(8,128)(2,1)} %bitcast.16, f32[64,128]{1,0:T(8,128)} %bitcast.20, s32[64,128]{1,0:T(8,128)} %bitcast.21), custom_call_target="tpu_custom_call" | custom-call | tf_op jit(solution)/shard_map/normal_operator/pallas_call | solution.py:337
  137.4 2.2 %copy.10 = bf16[1,512,2,256]{3,2,1,0:T(2,128)(2,1)} copy(bf16[1,512,2,256]{3,2,1,0:T(2,128)(2,1)} %bitcast.17) | data formatting | bytes 1048576
  139.6 1.8 %copy.11 = bf16[2,256,2,128]{3,2,1,0:T(2,128)(2,1)} copy(bf16[2,256,2,128]{3,2,1,0:T(2,128)(2,1)} %bitcast.19) | data formatting | bytes 524288

commit v4 on v3

--- a/solution.py
+++ b/solution.py
@@ -18,22 +18,24 @@
 GROUP = 4
 CHUNKS = TILES // GROUP
 STRIDE = 5
+OPPOSITE = next(s for s in range(TILES) if (s + 1) * STRIDE % TILES == 42)
 MESH = pl.DeviceIdType.MESH
 BF16 = jnp.bfloat16
 F32 = jnp.float32
 
 
-def offset_of(step):
+def nonzero(value):
+    return (value * value + 4095) // 4096
+
+
+def shifted(me, f, step, sign):
     mixed = lax.rem((step + 1) * STRIDE, TILES)
-    return mixed // 16, lax.rem(mixed // 4, 4), lax.rem(mixed, 4)
-
-
-def shifted(me, step, sign):
-    dy, dx, dz = offset_of(step)
+    dy, dx, dz = mixed // 16, lax.rem(mixed // 4, 4), lax.rem(mixed, 4)
+    more = 2 * f * nonzero(step - OPPOSITE) * nonzero(step - (TILES - 1)) + 4
     y, x, z = me // 16, lax.rem(me // 4, 4), lax.rem(me, 4)
-    y = lax.rem(y + sign * dy + 4, 4)
-    x = lax.rem(x + sign * dx + 4, 4)
-    z = lax.rem(z + sign * dz + 4, 4)
+    y = lax.rem(y + sign * dy + more, 4)
+    x = lax.rem(x + sign * dx + more, 4)
+    z = lax.rem(z + sign * dz + more, 4)
     return (y * 4 + x) * 4 + z
 
 
@@ -81,9 +83,9 @@
 
 def body(
     wave_hbm, col_hbm, row_hbm, scale_hbm, rank_hbm,
-    fwd_hbm, adj_hbm,
+    fwd_ref, adj_ref,
     scale_ref, rank_ref, vbuf, ubuf, waves, xmat, ybuf, send, recv, dense, acc,
-    stripes, fwdbuf, staying, leaving,
+    stripes, leaving,
     vsem, usem, ssem, rsem, xsems, lsems,
 ):
     me = lax.axis_index("tile")
@@ -104,11 +106,19 @@
         return pl.ds(pl.multiple_of(index * 2 * NB, 2 * NB), 2 * NB)
 
     barrier = pltpu.get_barrier_semaphore()
-    ys = [16 * lax.rem(me // 16 + k, 4) for k in range(4)]
-    xs = [4 * lax.rem(me // 4 + k, 4) for k in range(4)]
-    zs = [lax.rem(me + k, 4) for k in range(4)]
+    turned = [
+        (16 * lax.rem(me // 16 + more + k, 4), 4 * lax.rem(me // 4 + more + k, 4),
+         lax.rem(me + more + k, 4))
+        for more in (0, 2 * f) for k in range(4)
+    ]
     order = [(step + 1) * STRIDE % TILES for step in range(TILES)]
-    ids = [ys[at // 16] + xs[at // 4 % 4] + zs[at % 4] for at in order]
+    ids = []
+    for step, at in enumerate(order):
+        base = 0 if step in (OPPOSITE, last) else 4
+        ids.append(
+            turned[base + at // 16][0] + turned[base + at // 4 % 4][1]
+            + turned[base + at % 4][2]
+        )
     hops = [min(at // 16, 1) + min(at // 4 % 4, 1) + min(at % 4, 1)
             + (at // 16 == 2) + (at // 4 % 4 == 2) + (at % 4 == 2) for at in order]
     for step in sorted(range(last), key=lambda step: -hops[step]):
@@ -129,13 +139,13 @@
         u_copy(part).start()
 
     def targets(chunk, sign):
-        return [shifted(me, chunk * GROUP + k, sign) for k in range(GROUP)]
+        return [shifted(me, f, chunk * GROUP + k, sign) for k in range(GROUP)]
 
     def transfer(phase, step):
         return pltpu.make_async_remote_copy(
             src_ref=send.at[phase, step], dst_ref=recv.at[phase, step],
             send_sem=ssem.at[phase, step], recv_sem=rsem.at[phase, step],
-            device_id={"tile": shifted(me, step, 1)}, device_id_type=MESH,
+            device_id={"tile": shifted(me, f, step, 1)}, device_id_type=MESH,
         )
 
     def store(phase, chunk, values):
@@ -305,27 +315,32 @@
             at = 4 * NB * r + p
             stripes[pl.ds(at, NB, stride=4), :] = jnp.where(f == 0, own, other)
             stripes[pl.ds(at + 2, NB, stride=4), :] = jnp.where(f == 0, other, own)
-    fwdbuf[...] = stripes[...].astype(BF16)
-    fwd_copy = pltpu.make_async_copy(fwdbuf, fwd_hbm, lsems.at[3])
-    fwd_copy.start()
+    fwd_ref[...] = stripes[...].astype(BF16)
     sent(0)
     sent(1)
     expand_back(0)
-    merge(staying)
-    adj_copy = pltpu.make_async_copy(staying, adj_hbm.at[own_rows(f)], lsems.at[4])
-    adj_copy.start()
+    merge(adj_ref.at[own_rows(f)])
     expand_back(1)
     merge(leaving)
     out_copy = pltpu.make_async_remote_copy(
-        src_ref=leaving, dst_ref=adj_hbm.at[own_rows(f)], send_sem=xsems.at[2],
+        src_ref=leaving, dst_ref=adj_ref.at[own_rows(f)], send_sem=xsems.at[2],
         recv_sem=xsems.at[3], device_id=partner, device_id_type=MESH,
     )
     out_copy.start()
     sent(2)
     sent(3)
-    fwd_copy.wait()
-    adj_copy.wait()
     out_copy.wait()
+
+
+def hand_over(fwd_ref, adj_ref, fwd_hbm, adj_hbm, sems):
+    copies = [
+        pltpu.make_async_copy(fwd_ref, fwd_hbm, sems.at[0]),
+        pltpu.make_async_copy(adj_ref, adj_hbm, sems.at[1]),
+    ]
+    for copy in copies:
+        copy.start()
+    for copy in copies:
+        copy.wait()
 
 
 def per_device(wave_in, column_basis, row_basis, tile_scale, tile_ranks):
@@ -333,15 +348,16 @@
     columns = column_basis.reshape(TILES, 2, NB, WIDTH)
     rows = row_basis.reshape(2, TILES, NB, WIDTH)
     anywhere = pl.BlockSpec(memory_space=pl.ANY)
+    vmem = pl.BlockSpec(memory_space=pltpu.VMEM)
     packed = pltpu.VMEM((4, TILES, ROWS, HALF), BF16)
     forward, adjoint = pl.pallas_call(
         body,
         out_shape=(
-            jax.ShapeDtypeStruct((8 * NB, HALF), BF16),
-            jax.ShapeDtypeStruct((4 * NB, HALF), BF16),
+            pltpu.VMEM((8 * NB, HALF), BF16),
+            pltpu.VMEM((4 * NB, HALF), BF16),
         ),
         in_specs=[anywhere] * 5,
-        out_specs=(anywhere, anywhere),
+        out_specs=(vmem, vmem),
         scratch_shapes=[
             pltpu.SMEM((TILES, 2 * TILES), F32),
             pltpu.SMEM((TILES, 2 * TILES), jnp.int32),
@@ -354,21 +370,31 @@
             pltpu.VMEM((2 * GROUP * WIDTH, NVS), BF16),
             pltpu.VMEM((2, NB, NVS), F32),
             pltpu.VMEM((8 * NB, HALF), F32),
-            pltpu.VMEM((8 * NB, HALF), BF16),
-            pltpu.VMEM((2 * NB, HALF), BF16),
             pltpu.VMEM((2 * NB, HALF), BF16),
             pltpu.SemaphoreType.DMA((TILES,)),
             pltpu.SemaphoreType.DMA((4,)),
             pltpu.SemaphoreType.DMA((4, TILES)),
             pltpu.SemaphoreType.DMA((4, TILES)),
             pltpu.SemaphoreType.DMA((4,)),
-            pltpu.SemaphoreType.DMA((5,)),
+            pltpu.SemaphoreType.DMA((3,)),
         ],
         compiler_params=pltpu.CompilerParams(
             collective_id=0, has_side_effects=True, vmem_limit_bytes=56 << 20
         ),
         name="normal_operator",
     )(wave, columns, rows, tile_scale[0].T, tile_ranks[0].T)
+    forward, adjoint = pl.pallas_call(
+        hand_over,
+        out_shape=(
+            jax.ShapeDtypeStruct((8 * NB, HALF), BF16),
+            jax.ShapeDtypeStruct((4 * NB, HALF), BF16),
+        ),
+        in_specs=[vmem, vmem],
+        out_specs=(anywhere, anywhere),
+        scratch_shapes=[pltpu.SemaphoreType.DMA((2,))],
+        compiler_params=pltpu.CompilerParams(vmem_limit_bytes=4 << 20),
+        name="hand_over",
+    )(forward, adjoint)
     forward = forward.reshape(2 * NB, 2, 2, HALF).transpose(0, 2, 1, 3)
     forward_out = forward.reshape(1, 2 * NB, 2, NVS)
     adjoint_out = adjoint.reshape(2, NB, 2, HALF)

time: 143 us -> 158 us (1.10)
  the two profiles are of different devices: /device:TPU:1 before, /device:TPU:89 now
where the time goes in v4:
time: 158 us
  Pallas kernels  157 us (99%)
    pallas_call x1, Pallas kernels, per_device(): pl.pallas_call(body, out_shape=(pltpu.VMEM((8 * NB, HALF), BF16), pltpu.V...  156 us

profile of v4, /device:TPU:89, one launch (start us, length us, event | category | flops | bytes accessed | tf_op | source)
XLA Modules:
  0.0 157.5 jit_solution(5519564099668438885)
XLA Ops:
  0.6 156.0 %normal_operator.1 = (bf16[2048,128]{1,0:T(8,128)(2,1)S(1)}, bf16[1024,128]{1,0:T(8,128)(2,1)S(1)}) custom-call(bf16[1024,128]{1,0:T(8,128)(2,1)} %bitcast.17, bf16[64,2,256,128]{3,2,1,0:T(8,128)(2,1)} %bitcast.15, bf16[2,64,256,128]{3,2,1,0:T(8,128)(2,1)} %bitcast.16, f32[64,128]{1,0:T(8,128)} %bitcast.18, s32[64,128]{1,0:T(8,128)} %bitcast.19), custom_call_target="tpu_custom_call" | custom-call | tf_op jit(solution)/shard_map/normal_operator/pallas_call | solution.py:353
  156.6 0.9 hand_over.1

commit v5 on v4

--- a/solution.py
+++ b/solution.py
@@ -17,25 +17,23 @@
 ROWS = 32 * SLOTS
 GROUP = 4
 CHUNKS = TILES // GROUP
-STRIDE = 5
-OPPOSITE = next(s for s in range(TILES) if (s + 1) * STRIDE % TILES == 42)
+STRIDE = 27
 MESH = pl.DeviceIdType.MESH
 BF16 = jnp.bfloat16
 F32 = jnp.float32
 
 
-def nonzero(value):
-    return (value * value + 4095) // 4096
-
-
-def shifted(me, f, step, sign):
+def offset_of(step):
     mixed = lax.rem((step + 1) * STRIDE, TILES)
-    dy, dx, dz = mixed // 16, lax.rem(mixed // 4, 4), lax.rem(mixed, 4)
-    more = 2 * f * nonzero(step - OPPOSITE) * nonzero(step - (TILES - 1)) + 4
+    return mixed // 16, lax.rem(mixed // 4, 4), lax.rem(mixed, 4)
+
+
+def shifted(me, step, sign):
+    dy, dx, dz = offset_of(step)
     y, x, z = me // 16, lax.rem(me // 4, 4), lax.rem(me, 4)
-    y = lax.rem(y + sign * dy + more, 4)
-    x = lax.rem(x + sign * dx + more, 4)
-    z = lax.rem(z + sign * dz + more, 4)
+    y = lax.rem(y + sign * dy + 4, 4)
+    x = lax.rem(x + sign * dx + 4, 4)
+    z = lax.rem(z + sign * dz + 4, 4)
     return (y * 4 + x) * 4 + z
 
 
@@ -106,19 +104,11 @@
         return pl.ds(pl.multiple_of(index * 2 * NB, 2 * NB), 2 * NB)
 
     barrier = pltpu.get_barrier_semaphore()
-    turned = [
-        (16 * lax.rem(me // 16 + more + k, 4), 4 * lax.rem(me // 4 + more + k, 4),
-         lax.rem(me + more + k, 4))
-        for more in (0, 2 * f) for k in range(4)
-    ]
+    ys = [16 * lax.rem(me // 16 + k, 4) for k in range(4)]
+    xs = [4 * lax.rem(me // 4 + k, 4) for k in range(4)]
+    zs = [lax.rem(me + k, 4) for k in range(4)]
     order = [(step + 1) * STRIDE % TILES for step in range(TILES)]
-    ids = []
-    for step, at in enumerate(order):
-        base = 0 if step in (OPPOSITE, last) else 4
-        ids.append(
-            turned[base + at // 16][0] + turned[base + at // 4 % 4][1]
-            + turned[base + at % 4][2]
-        )
+    ids = [ys[at // 16] + xs[at // 4 % 4] + zs[at % 4] for at in order]
     hops = [min(at // 16, 1) + min(at // 4 % 4, 1) + min(at % 4, 1)
             + (at // 16 == 2) + (at // 4 % 4 == 2) + (at % 4 == 2) for at in order]
     for step in sorted(range(last), key=lambda step: -hops[step]):
@@ -139,13 +129,13 @@
         u_copy(part).start()
 
     def targets(chunk, sign):
-        return [shifted(me, f, chunk * GROUP + k, sign) for k in range(GROUP)]
+        return [shifted(me, chunk * GROUP + k, sign) for k in range(GROUP)]
 
     def transfer(phase, step):
         return pltpu.make_async_remote_copy(
             src_ref=send.at[phase, step], dst_ref=recv.at[phase, step],
             send_sem=ssem.at[phase, step], recv_sem=rsem.at[phase, step],
-            device_id={"tile": shifted(me, f, step, 1)}, device_id_type=MESH,
+            device_id={"tile": shifted(me, step, 1)}, device_id_type=MESH,
         )
 
     def store(phase, chunk, values):

time: 158 us -> 138 us (0.87)
  the two profiles are of different devices: /device:TPU:89 before, /device:TPU:1 now
where the time goes in v5:
time: 138 us
  Pallas kernels  137 us (99%)
    pallas_call x1, Pallas kernels, per_device(): pl.pallas_call(body, out_shape=(pltpu.VMEM((8 * NB, HALF), BF16), pltpu.V...  136 us

profile of v5, /device:TPU:1, one launch (start us, length us, event | category | flops | bytes accessed | tf_op | source)
XLA Modules:
  0.0 137.8 jit_solution(2005607282843954037)
XLA Ops:
  0.6 136.3 %normal_operator.1 = (bf16[2048,128]{1,0:T(8,128)(2,1)S(1)}, bf16[1024,128]{1,0:T(8,128)(2,1)S(1)}) custom-call(bf16[1024,128]{1,0:T(8,128)(2,1)} %bitcast.17, bf16[64,2,256,128]{3,2,1,0:T(8,128)(2,1)} %bitcast.15, bf16[2,64,256,128]{3,2,1,0:T(8,128)(2,1)} %bitcast.16, f32[64,128]{1,0:T(8,128)} %bitcast.18, s32[64,128]{1,0:T(8,128)} %bitcast.19), custom_call_target="tpu_custom_call" | custom-call | tf_op jit(solution)/shard_map/normal_operator/pallas_call | solution.py:343
  136.9 0.9 hand_over.1

commit v6 on v5

--- a/solution.py
+++ b/solution.py
@@ -162,6 +162,14 @@
         def _():
             transfer(phase, chunk * GROUP + GROUP - 1).wait_recv()
 
+    def settle(phase, chunk):
+        for k in range(GROUP - 1):
+            transfer(phase, chunk * GROUP + k).wait_send()
+
+        @pl.when(chunk < CHUNKS - 1)
+        def _():
+            transfer(phase, chunk * GROUP + GROUP - 1).wait_send()
+
     def sent(phase):
         @pl.loop(0, last)
         def _(step):
@@ -238,8 +246,6 @@
             depart(2 + half, chunk)
 
     def expand_back(half):
-        acc[0] = jnp.zeros((NB, NVS), F32)
-
         @pl.loop(0, CHUNKS)
         def _(chunk):
             arrive(2 + half, chunk)
@@ -252,7 +258,8 @@
                 dense[2 * k * WIDTH : (2 * k + 1) * WIDTH] = first
                 dense[(2 * k + 1) * WIDTH : (2 * k + 2) * WIDTH] = second
             left = jnp.concatenate([vbuf[d, r] for d in ids for r in range(2)], 1)
-            acc[0] += jnp.dot(left, dense[...], preferred_element_type=F32)
+            acc[half] += jnp.dot(left, dense[...], preferred_element_type=F32)
+            settle(2 + half, chunk)
 
     def split(half):
         stripes[: 2 * NB] = waves[half].astype(F32)
@@ -260,9 +267,10 @@
             part = stripes[pl.ds(p, NB, stride=2), :]
             xmat[half, :, p * HALF : (p + 1) * HALF] = part.astype(BF16)
 
-    def merge(target):
+    def merge(half, target):
         for p in range(2):
-            stripes[pl.ds(p, NB, stride=2), :] = acc[0, :, p * HALF : (p + 1) * HALF]
+            part = acc[half, :, p * HALF : (p + 1) * HALF]
+            stripes[pl.ds(p, NB, stride=2), :] = part
         target[...] = stripes[: 2 * NB].astype(BF16)
 
     for copy in table_copies:
@@ -308,17 +316,16 @@
     fwd_ref[...] = stripes[...].astype(BF16)
     sent(0)
     sent(1)
+    acc[...] = jnp.zeros_like(acc)
     expand_back(0)
-    merge(adj_ref.at[own_rows(f)])
     expand_back(1)
-    merge(leaving)
+    merge(1, leaving)
     out_copy = pltpu.make_async_remote_copy(
         src_ref=leaving, dst_ref=adj_ref.at[own_rows(f)], send_sem=xsems.at[2],
         recv_sem=xsems.at[3], device_id=partner, device_id_type=MESH,
     )
     out_copy.start()
-    sent(2)
-    sent(3)
+    merge(0, adj_ref.at[own_rows(f)])
     out_copy.wait()
 
 

time: 138 us -> 138 us (level)
  no operation moved by 1% of the time
where the time goes in v6:
time: 138 us
  Pallas kernels  137 us (99%)
    pallas_call x1, Pallas kernels, per_device(): pl.pallas_call(body, out_shape=(pltpu.VMEM((8 * NB, HALF), BF16), pltpu.V...  136 us

profile of v6, /device:TPU:1, one launch (start us, length us, event | category | flops | bytes accessed | tf_op | source)
XLA Modules:
  0.0 137.8 jit_solution(3032554190578793792)
XLA Ops:
  0.6 136.3 %normal_operator.1 = (bf16[2048,128]{1,0:T(8,128)(2,1)S(1)}, bf16[1024,128]{1,0:T(8,128)(2,1)S(1)}) custom-call(bf16[1024,128]{1,0:T(8,128)(2,1)} %bitcast.17, bf16[64,2,256,128]{3,2,1,0:T(8,128)(2,1)} %bitcast.15, bf16[2,64,256,128]{3,2,1,0:T(8,128)(2,1)} %bitcast.16, f32[64,128]{1,0:T(8,128)} %bitcast.18, s32[64,128]{1,0:T(8,128)} %bitcast.19), custom_call_target="tpu_custom_call" | custom-call | tf_op jit(solution)/shard_map/normal_operator/pallas_call | solution.py:350
  137.0 0.9 hand_over.1

commit v7 on v6

--- a/solution.py
+++ b/solution.py
@@ -17,7 +17,7 @@
 ROWS = 32 * SLOTS
 GROUP = 4
 CHUNKS = TILES // GROUP
-STRIDE = 27
+STRIDE = 35
 MESH = pl.DeviceIdType.MESH
 BF16 = jnp.bfloat16
 F32 = jnp.float32

time: 138 us -> 138 us (level)
  no operation moved by 1% of the time
where the time goes in v7:
time: 138 us
  Pallas kernels  137 us (99%)
    pallas_call x1, Pallas kernels, per_device(): pl.pallas_call(body, out_shape=(pltpu.VMEM((8 * NB, HALF), BF16), pltpu.V...  136 us

profile of v7, /device:TPU:1, one launch (start us, length us, event | category | flops | bytes accessed | tf_op | source)
XLA Modules:
  0.0 137.6 jit_solution(11279504854480259034)
XLA Ops:
  0.6 136.0 %normal_operator.1 = (bf16[2048,128]{1,0:T(8,128)(2,1)S(1)}, bf16[1024,128]{1,0:T(8,128)(2,1)S(1)}) custom-call(bf16[1024,128]{1,0:T(8,128)(2,1)} %bitcast.17, bf16[64,2,256,128]{3,2,1,0:T(8,128)(2,1)} %bitcast.15, bf16[2,64,256,128]{3,2,1,0:T(8,128)(2,1)} %bitcast.16, f32[64,128]{1,0:T(8,128)} %bitcast.18, s32[64,128]{1,0:T(8,128)} %bitcast.19), custom_call_target="tpu_custom_call" | custom-call | tf_op jit(solution)/shard_map/normal_operator/pallas_call | solution.py:350
  136.7 0.9 hand_over.1
